TPU v7x, 32 devices: a whole 2x2x4 slice. The times are simulated.
32 devices in a mesh: seq: 8 (over z, y), tp: 4 (over x, core).
Axes of the slice: x: 2, y: 2, z: 4, core: 2. Of those that a mesh axis runs over, the one named last changes fastest.
Arguments:
- states: bfloat16 [2048, 1536], P('seq', 'tp')
- modulation: float32 [3, 1536], replicated, may hold values from -2.5 to 2.5
- query_weight: bfloat16 [1536, 1536], P(None, 'tp')
- key_weight: bfloat16 [1536, 1536], P(None, 'tp')
- value_weight: bfloat16 [1536, 1536], P(None, 'tp'), may hold values from -0.15625 to 0.15625
- out_weight: bfloat16 [1536, 1536], P(None, 'tp'), may hold values from -0.15625 to 0.15625
- pattern: int32 [16, 7], replicated, may hold values from 0 to 15, as said below
Outputs:
- updated: bfloat16 [2048, 1536], P('seq', 'tp')
Inputs may be any that keep to these rules, and one draw needn't show every extreme that they name: `pattern`: the 2 query tiles 2 d to 2 d + 1 list the same set of 7 distinct tiles, each in an order of its own: all tiles 2 d to 2 d + 1, and exactly one tile from each of 5 other groups of 2 tiles (group e being tiles 2 e to 2 e + 1).
All inputs are finite; a program needn't handle non-finite values.
Results may differ from a plain program's by a relative error of at most 0.0056.
Values may be sent and summed in bfloat16 or wider, within the bound.
A program may use at most 128 MiB of HBM per device.

v0:
```python
import math

import jax
import jax.numpy as jnp
from jax import lax
from jax.sharding import PartitionSpec as P

HD = 128
TILE = 128


def local(states, modulation, query_weight, key_weight, value_weight, out_weight, pattern):
    tok_rows, local_cols = states.shape
    col_start = lax.axis_index("tp") * local_cols
    mod_cols = lax.dynamic_slice_in_dim(modulation, col_start, local_cols, 1)
    states_f = states.astype(jnp.float32)
    gathered = lax.all_gather(states, "tp", axis=1, tiled=True)
    gathered_f = gathered.astype(jnp.float32)
    row_mean = jnp.mean(gathered_f, axis=1, keepdims=True)
    centered = gathered_f - row_mean
    variance = jnp.mean(centered * centered, axis=1, keepdims=True)
    normed = (
        centered * lax.rsqrt(variance + 1e-06) * (1.0 + modulation[1]) + modulation[0]
    ).astype(jnp.bfloat16)
    query = jnp.dot(normed, query_weight, preferred_element_type=jnp.float32).astype(jnp.bfloat16)
    keys = jnp.dot(normed, key_weight, preferred_element_type=jnp.float32).astype(jnp.bfloat16)
    values = jnp.dot(normed, value_weight, preferred_element_type=jnp.float32).astype(jnp.bfloat16)
    head_cols = query.shape[1]
    heads_local = head_cols // HD
    key_value = jnp.concatenate([keys, values], axis=1)
    tiles_dev = tok_rows // TILE
    devices = lax.axis_size("seq")
    seq_index = lax.axis_index("seq")
    list_count = pattern.shape[1]
    groups = pattern.reshape(devices, tiles_dev, list_count)
    first_lists = groups[:, 0, :]
    my_list = lax.dynamic_index_in_dim(first_lists, seq_index, 0, keepdims=False)
    all_tiles = lax.all_gather(key_value, "seq", axis=0, tiled=True)
    tile_store = all_tiles.reshape(devices * tiles_dev, TILE, 2 * head_cols)
    listed_rows = jnp.take(tile_store, my_list, axis=0).reshape(
        list_count * TILE, 2, heads_local, HD
    )
    key_rows = listed_rows[:, 0]
    value_rows = listed_rows[:, 1]
    factor = 1.0 / math.sqrt(HD)
    block_rows = min(512, tok_rows)
    block_count = tok_rows // block_rows

    def attend(query_block):
        scores = (
            jnp.einsum("qhd,khd->hqk", query_block, key_rows, preferred_element_type=jnp.float32)
            * factor
        )
        row_max = jnp.max(scores, axis=2, keepdims=True)
        weights_full = jnp.exp(scores - row_max)
        weight_sum = jnp.sum(weights_full, axis=2)
        weights = weights_full.astype(jnp.bfloat16)
        summed = jnp.einsum("hqk,khd->qhd", weights, value_rows, preferred_element_type=jnp.float32)
        return (summed / jnp.transpose(weight_sum)[:, :, None]).astype(jnp.bfloat16)

    query_blocks = query.reshape(block_count, block_rows, heads_local, HD)
    attended = lax.map(attend, query_blocks).reshape(tok_rows, head_cols)
    projected = jnp.dot(
        lax.all_gather(attended, "tp", axis=1, tiled=True),
        out_weight,
        preferred_element_type=jnp.float32,
    )
    return (states_f + mod_cols[2] * projected).astype(jnp.bfloat16)


def solution(mesh):
    placed = (P("seq", "tp"), P(), P(None, "tp"), P(None, "tp"), P(None, "tp"), P(None, "tp"), P())
    return jax.shard_map(
        local, mesh=mesh, in_specs=placed, out_specs=P("seq", "tp"), check_vma=False
    )
```

profile of v0, /device:TPU:0, one launch (start us, length us, event | category | flops | bytes accessed | tf_op | source)
XLA Modules:
  0.0 108.7 jit_solution(18333908711656933639)
XLA Ops:
  6.5 0.0 copy-start
  6.5 0.0 all-gather.2.cloned.1.call-start
  6.5 0.9 add_reduce_fusion
  7.4 10.3 %all_gather.9 = bf16[256,1536]{1,0:T(8,128)(2,1)S(1)} all-gather(bf16[256,384]{1,0:T(8,128)(2,1)} %param.7), channel_id=1, replica_groups=mesh['seq'=8,'tp'=4] {'tp'}, dimensions={1}, use_global_device_ids=true | all-gather | bytes 983040 | tf_op jit(solution)/shard_map/all_gather | solution.py:17
  17.7 0.2 convert_reduce_fusion
  17.9 0.3 fusion.4
  18.3 0.0 copy-done
  18.3 0.0 copy-start.3
  18.3 0.6 convolution_convert_fusion.1
  18.9 0.6 copy-done.3
  19.6 0.0 copy-start.2
  19.6 0.0 copy-start.4
  19.6 0.6 convolution_convert_fusion.2
  20.2 0.8 pad_maximum_fusion
  21.0 0.0 all-gather.2.cloned.1.call-update
  21.0 0.0 copy-done.2
  21.0 0.1 copy.16
  21.1 0.0 copy-done.4
  21.1 0.7 convolution_convert_fusion
  21.8 0.1 copy.19
  21.9 0.8 dynamic-slice_reduce_fusion
  22.7 0.1 broadcast_bitcast_fusion
  22.8 59.2 %all-gather.2.cloned.1.call-done = bf16[2048,768]{1,0:T(8,128)(2,1)} async-done(((bf16[256,768]{1,0:T(8,128)(2,1)}), bf16[2048,768]{1,0:T(8,128)(2,1)}) %all-gather.2.cloned.1.call-update) | async-done | bytes 3145744 | tf_op jit(solution)/shard_map/all_gather | solution.py:38
  82.0 3.6 %gather_fusion = bf16[7,128,768]{2,1,0:T(8,128)(2,1)} fusion(bf16[16,128,768]{2,1,0:T(8,128)(2,1)} %bitcast.34, s32[1024]{0:T(1024)S(1)} %pad_clamp_fusion), kind=kCustom, calls=%fused_computation | custom fusion | bytes 2752540 | tf_op jit(solution)/shard_map/jit(_take)/gather | solution.py:40
  85.6 3.9 %reshape.76 = bf16[896,2,3,128]{3,2,1,0:T(4,128)(2,1)S(1)} reshape(bf16[7,128,768]{2,1,0:T(8,128)(2,1)} %gather_fusion) | data formatting | bytes 2752512 | tf_op jit(solution)/shard_map/jit(_take)/gather | solution.py:40
  89.5 0.3 copy_select_fusion
  89.8 0.7 multiply_reduce_fusion
  90.5 0.7 fusion
  91.1 0.0 copy-start.1
  91.1 0.0 copy-start.5
  91.1 0.8 fusion.19
  92.0 8.6 %all_gather.11 = bf16[256,1536]{0,1:T(8,128)(2,1)S(1)} all-gather(bf16[256,384]{0,1:T(8,128)(2,1)S(1)} %bitcast.35), channel_id=1, replica_groups=mesh['seq'=8,'tp'=4] {'tp'}, dimensions={1}, use_global_device_ids=true | all-gather | bytes 983040 | tf_op jit(solution)/shard_map/all_gather | solution.py:64
  100.5 0.0 copy-done.1
  100.5 0.0 copy-done.5
  100.5 1.3 %fusion.22 = bf16[256,384]{1,0:T(8,128)(2,1)} fusion(bf16[256,1536]{0,1:T(8,128)(2,1)S(1)} %all_gather.11, bf16[1536,384]{1,0:T(8,128)(2,1)S(1)} %copy-done.5, bf16[256,384]{1,0:T(8,128)(2,1)S(1)} %copy-done.1, f32[384]{0:T(512)S(1)} %dynamic-slice_reduce_fusion), kind=kOutput, calls=%fused_computation.25 | convolution fusion | flops 302383104 | bytes 2360832 | tf_op jit(solution)/shard_map/dot_general | solution.py:63
  (6 shorter events, 0.0 us)
Async XLA Ops:
  6.5 11.7 %copy-start = (bf16[1536,384]{1,0:T(8,128)(2,1)S(1)}, bf16[1536,384]{1,0:T(8,128)(2,1)}, u32[]{:S(2)}) copy-start(bf16[1536,384]{1,0:T(8,128)(2,1)} %param.11) | copy-start | bytes 3538948
  6.5 75.5 %all-gather.2.cloned.1.call-start = ((), (), s32[]{:S(2)}) async-start(), calls=%async_computation | async-start | bytes 3538944 | tf_op jit(solution)/shard_map/all_gather | solution.py:38
  18.3 1.3 %copy-start.3 = (bf16[1536,384]{1,0:T(8,128)(2,1)S(1)}, bf16[1536,384]{1,0:T(8,128)(2,1)}, u32[]{:S(2)}) copy-start(bf16[1536,384]{1,0:T(8,128)(2,1)} %param.10) | copy-start | bytes 3538948
  19.6 1.4 %copy-start.2 = (s32[16,7]{0,1:T(8,128)S(1)}, s32[16,7]{0,1:T(8,128)}, u32[]{:S(2)}) copy-start(s32[16,7]{0,1:T(8,128)} %param.13) | copy-start | bytes 1348
  19.6 1.5 %copy-start.4 = (bf16[1536,384]{1,0:T(8,128)(2,1)S(1)}, bf16[1536,384]{1,0:T(8,128)(2,1)}, u32[]{:S(2)}) copy-start(bf16[1536,384]{1,0:T(8,128)(2,1)} %param.9) | copy-start | bytes 3538948
  91.1 9.4 %copy-start.1 = (bf16[256,384]{1,0:T(8,128)(2,1)S(1)}, bf16[256,384]{1,0:T(8,128)(2,1)}, u32[]{:S(2)}) copy-start(bf16[256,384]{1,0:T(8,128)(2,1)} %param.7) | copy-start | bytes 589828
  91.1 9.4 %copy-start.5 = (bf16[1536,384]{1,0:T(8,128)(2,1)S(1)}, bf16[1536,384]{1,0:T(8,128)(2,1)}, u32[]{:S(2)}) copy-start(bf16[1536,384]{1,0:T(8,128)(2,1)} %param.12) | copy-start | bytes 3538948
Sparse Core Ops, SparseCore 0:
  21.1 60.8 all-gather.1
where the time goes:
time: 109 us
  waiting for transfers between devices  59.2 us (54%)
  blocking collectives  18.9 us (17%)
  between operations  13.5 us (12%)
  local copies, waits for them, and re-layouts  9.24 us (8%)
  matrix products  4.7 us (4%)
  other arithmetic  3.14 us (3%)
    all_gather x1, waiting for transfers between devices, local(): all_tiles = lax.all_gather(key_value, 'seq', axis=0, tiled=True)  59.2 us
    all_gather x1, blocking collectives, local(): gathered = lax.all_gather(states, 'tp', axis=1, tiled=True)  10.3 us
    all_gather x1, blocking collectives, local(): lax.all_gather(attended, 'tp', axis=1, tiled=True)  8.58 us
    gather x2, local copies, waits for them, and re-layouts, local(): jnp.take(tile_store, my_list, axis=0)  7.5 us
  transfers between devices with their start and end apart: 1, of which 1 were waited for; matrix products, arithmetic and copies ran while one was open for 2% of the time, Pallas kernels for 0%

commit v1 on v0

--- a/solution.py
+++ b/solution.py
@@ -3,10 +3,340 @@
 import jax
 import jax.numpy as jnp
 from jax import lax
+from jax.experimental import pallas as pl
+from jax.experimental.pallas import tpu as pltpu
 from jax.sharding import PartitionSpec as P
 
 HD = 128
 TILE = 128
+MESH = pl.DeviceIdType.MESH
+F32 = jnp.float32
+BF16 = jnp.bfloat16
+
+
+def fused_kernel(
+    pat, x_ref, mod, wq_hbm, wk_hbm, wv_hbm, wo_hbm, o_ref,
+    zb, ys, yr, gat, att, wq, wk, wv, wo, nb, qb, kb, vb, sc,
+    wsem, zup, zdn, zfw, zrv, ysn, yrv, xsn, xrv, csn, crv, dsn, drv,
+    axs, axr, acs, acr, ads, adr,
+):
+    seq, tp = lax.axis_index("seq"), lax.axis_index("tp")
+    z, y = seq // 2, seq % 2
+    xx, c = tp // 2, tp % 2
+    half = z // 2
+    zz = z + half * (3 - 2 * z)
+    step = 1 - 2 * half
+    up = ((z + step) * 2 + y, tp)
+    down = ((z - step) * 2 + y, tp)
+    yp = (z * 2 + 1 - y, tp)
+    tx = (1 - xx) * 2 + c
+    tc = xx * 2 + 1 - c
+    td = (1 - xx) * 2 + 1 - c
+    xp = (seq, tx)
+    cp = (seq, tc)
+    cols = x_ref.shape[1]
+    inner = zz == 1
+
+    def remote(src, dst, ss, rs, dev):
+        return pltpu.make_async_remote_copy(
+            src_ref=src, dst_ref=dst, send_sem=ss, recv_sem=rs, device_id=dev, device_id_type=MESH
+        )
+
+    loads = [
+        pltpu.make_async_copy(a, b, wsem.at[i])
+        for i, (a, b) in enumerate(((wq_hbm, wq), (wk_hbm, wk), (wv_hbm, wv), (wo_hbm, wo)))
+    ]
+    for cpy in loads:
+        cpy.start()
+
+    barrier = pltpu.get_barrier_semaphore()
+    for dev in (up, yp, xp, cp):
+        pl.semaphore_signal(barrier, inc=1, device_id=dev, device_id_type=MESH)
+
+    @pl.when(inner)
+    def _():
+        pl.semaphore_signal(barrier, inc=1, device_id=down, device_id_type=MESH)
+
+    pl.semaphore_wait(barrier, 4 + zz)
+
+    def own(t):
+        return x_ref.at[pl.ds(t * TILE, TILE)]
+
+    def z_own_up(t):
+        return remote(own(t), zb.at[zz, t], zup.at[t], zrv.at[zz * 2 + t], up)
+
+    def z_own_down(t):
+        return remote(own(t), zb.at[0, t], zdn.at[t], zrv.at[t], down)
+
+    def z_forward(i, t):
+        if i == 0:
+            return remote(zb.at[0, t], zb.at[2, t], zfw.at[t], zrv.at[4 + t], up)
+        return remote(zb.at[i, t], zb.at[i, t], zfw.at[i * 2 + t], zrv.at[i * 2 + t], down)
+
+    def z_arrive(i, t):
+        remote(zb.at[i, t], zb.at[i, t], zfw.at[i * 2 + t], zrv.at[i * 2 + t], up).wait_recv()
+
+        @pl.when(inner)
+        def _():
+            z_forward(i, t).start()
+
+    def y_copy(i):
+        return remote(ys.at[i], yr.at[i], ysn.at[i], yrv.at[i], yp)
+
+    def x_copy(k):
+        src = own(k) if k < 2 else gat.at[tp, k]
+        return remote(src, gat.at[tp, k], xsn.at[k], xrv.at[k], xp)
+
+    def c_copy(k):
+        src = own(k) if k < 2 else gat.at[tp, k]
+        return remote(src, gat.at[tp, k], csn.at[k], crv.at[k], cp)
+
+    def d_copy(k):
+        return remote(gat.at[tx, k], gat.at[tx, k], dsn.at[k], drv.at[k], cp)
+
+    def x_arrive(k):
+        remote(gat.at[tx, k], gat.at[tx, k], xsn.at[k], xrv.at[k], xp).wait_recv()
+        d_copy(k).start()
+
+    def rest_arrive(k):
+        remote(gat.at[tc, k], gat.at[tc, k], csn.at[k], crv.at[k], cp).wait_recv()
+        remote(gat.at[td, k], gat.at[td, k], dsn.at[k], drv.at[k], cp).wait_recv()
+
+    for t in range(2):
+        z_own_up(t).start()
+
+        @pl.when(inner)
+        def _():
+            z_own_down(t).start()
+
+        x_copy(t).start()
+        c_copy(t).start()
+
+    def place(i):
+        at = (z, 1 - zz, 2, 3)[i]
+        return at if i == 0 else at + half * (3 - 2 * at)
+
+    lists = pat.shape[1]
+    mine = [pat[2 * seq, n] for n in range(lists)]
+    theirs = [pat[2 * (z * 2 + 1 - y), n] for n in range(lists)]
+
+    def count(entries, value):
+        return sum(jnp.where(e == value, 1, 0) for e in entries)
+
+    def y_stage(i):
+        odd = count(theirs, 2 * (place(i) * 2 + y) + 1)
+        if i == 0:
+            first, second = x_ref[0:TILE], x_ref[TILE:]
+        else:
+            first, second = zb[i - 1, 0], zb[i - 1, 1]
+        ys[i] = lax.select(odd == 1, second, first)
+        y_copy(i).start()
+
+    cands = []
+    rank = 0
+    for i in range(4):
+        for from_y in ((True,) if i == 0 else (False, True)):
+            group = place(i) * 2 + ((1 - y) if from_y else y)
+            even, odd = count(mine, 2 * group), count(mine, 2 * group + 1)
+            cands.append((i, from_y, even, odd, rank))
+            rank = rank + even + odd
+
+    def slot_stage(k):
+        value = None
+        for j in range(k, k + 3):
+            i, from_y, even, odd, place_of = cands[j]
+            if from_y:
+                options = [(even + odd, yr[i])]
+            else:
+                options = [(even, zb[i - 1, 0]), (odd, zb[i - 1, 1])]
+            for listed, tile in options:
+                if value is None:
+                    value = tile
+                else:
+                    here = jnp.where(place_of == k, listed, 0)
+                    value = lax.select(here == 1, tile, value)
+        gat[tp, 2 + k] = value
+        x_copy(2 + k).start()
+        c_copy(2 + k).start()
+
+    def normalize(k, row):
+        blocks = [gat[t, k].astype(F32) for t in range(4)]
+        width = 4 * cols
+        mean = sum(jnp.sum(b, axis=1, keepdims=True) for b in blocks) / width
+        blocks = [b - mean for b in blocks]
+        var = sum(jnp.sum(b * b, axis=1, keepdims=True) for b in blocks) / width
+        scale = lax.rsqrt(var + 1e-06)
+        for t in range(4):
+            lanes = slice(t * cols, (t + 1) * cols)
+            nb[row : row + TILE, lanes] = (
+                blocks[t] * scale * (1.0 + mod[1:2, lanes]) + mod[0:1, lanes]
+            ).astype(BF16)
+
+    heads = cols // HD
+    factor = 1.0 / math.sqrt(HD)
+
+    def project(first, rows):
+        normed = nb[0:rows]
+        at = first * TILE
+        kb[at : at + rows] = jnp.dot(normed, wk[...], preferred_element_type=F32).astype(BF16)
+        for h in range(heads):
+            lanes = slice(h * HD, (h + 1) * HD)
+            sc[h, :, at : at + rows] = (
+                lax.dot_general(
+                    qb[:, lanes], kb[at : at + rows, lanes], (((1,), (1,)), ((), ())),
+                    preferred_element_type=F32,
+                )
+                * factor
+            )
+        vb[at : at + rows] = jnp.dot(normed, wv[...], preferred_element_type=F32).astype(BF16)
+
+    def attend(k):
+        rest_arrive(k)
+        normalize(k, 0)
+        project(k, TILE)
+
+    y_stage(0)
+    for t in range(2):
+        z_arrive(0, t)
+        gat[tp, t] = x_ref[t * TILE : (t + 1) * TILE]
+        x_arrive(t)
+    y_stage(1)
+    for t in range(2):
+        rest_arrive(t)
+        normalize(t, t * TILE)
+    for cpy in loads[:3]:
+        cpy.wait()
+    qb[...] = jnp.dot(nb[...], wq[...], preferred_element_type=F32).astype(BF16)
+    project(0, 2 * TILE)
+
+    def y_arrive(i):
+        y_copy(i).wait_recv()
+
+    y_arrive(0)
+    y_arrive(1)
+    slot_stage(0)
+    z_arrive(1, 0)
+    z_arrive(1, 1)
+    y_stage(2)
+    slot_stage(1)
+    x_arrive(2)
+    z_arrive(2, 0)
+    x_arrive(3)
+    z_arrive(2, 1)
+    y_stage(3)
+    y_arrive(2)
+    slot_stage(2)
+    slot_stage(3)
+    attend(2)
+    y_arrive(3)
+    slot_stage(4)
+    x_arrive(4)
+    attend(3)
+    x_arrive(5)
+    attend(4)
+    x_arrive(6)
+    attend(5)
+    attend(6)
+
+    def att_part(t, h):
+        return att.at[t, :, pl.ds(h * HD, HD)]
+
+    def ax_copy(h):
+        return remote(att_part(tp, h), att_part(tp, h), axs.at[h], axr.at[h], xp)
+
+    def ac_copy(h):
+        return remote(att_part(tp, h), att_part(tp, h), acs.at[h], acr.at[h], cp)
+
+    def ad_copy(h):
+        return remote(att_part(tx, h), att_part(tx, h), ads.at[h], adr.at[h], cp)
+
+    for h in range(heads):
+        lanes = slice(h * HD, (h + 1) * HD)
+        scores = sc[h]
+        full = jnp.exp(scores - jnp.max(scores, axis=1, keepdims=True))
+        total = jnp.sum(full, axis=1, keepdims=True)
+        summed = jnp.dot(full.astype(BF16), vb[:, lanes], preferred_element_type=F32)
+        att[tp, :, lanes] = (summed / total).astype(BF16)
+        ax_copy(h).start()
+        ac_copy(h).start()
+
+    loads[3].wait()
+    acc = jnp.dot(att[tp], wo[tp], preferred_element_type=F32)
+    for h in range(heads):
+        remote(att_part(tx, h), att_part(tx, h), axs.at[h], axr.at[h], xp).wait_recv()
+        ad_copy(h).start()
+    for h in range(heads):
+        remote(att_part(tc, h), att_part(tc, h), acs.at[h], acr.at[h], cp).wait_recv()
+    acc = acc + jnp.dot(att[tc], wo[tc], preferred_element_type=F32)
+    acc = acc + jnp.dot(att[tx], wo[tx], preferred_element_type=F32)
+    for h in range(heads):
+        remote(att_part(td, h), att_part(td, h), ads.at[h], adr.at[h], cp).wait_recv()
+    acc = acc + jnp.dot(att[td], wo[td], preferred_element_type=F32)
+    gate = mod[2:3, pl.ds(pl.multiple_of(tp * cols, HD), cols)]
+    o_ref[...] = (x_ref[...].astype(F32) + gate * acc).astype(BF16)
+
+    for t in range(2):
+        z_own_up(t).wait_send()
+
+        @pl.when(inner)
+        def _():
+            z_own_down(t).wait_send()
+            for i in range(3):
+                z_forward(i, t).wait_send()
+
+    for i in range(4):
+        y_copy(i).wait_send()
+    for k in range(lists):
+        x_copy(k).wait_send()
+        c_copy(k).wait_send()
+        d_copy(k).wait_send()
+    for h in range(heads):
+        ax_copy(h).wait_send()
+        ac_copy(h).wait_send()
+        ad_copy(h).wait_send()
+
+
+def fused(states, modulation, query_weight, key_weight, value_weight, out_weight, pattern):
+    rows, cols = states.shape
+    width = modulation.shape[1]
+    lists = pattern.shape[1]
+    heads = cols // HD
+    vmem = pl.BlockSpec(memory_space=pltpu.VMEM)
+    hbm = pl.BlockSpec(memory_space=pl.ANY)
+    dma = pltpu.SemaphoreType.DMA
+    return pl.pallas_call(
+        fused_kernel,
+        out_shape=jax.ShapeDtypeStruct((rows, cols), BF16),
+        in_specs=[pl.BlockSpec(memory_space=pltpu.SMEM), vmem, vmem, hbm, hbm, hbm, hbm],
+        out_specs=vmem,
+        scratch_shapes=[
+            pltpu.VMEM((3, 2, TILE, cols), BF16),
+            pltpu.VMEM((4, TILE, cols), BF16),
+            pltpu.VMEM((4, TILE, cols), BF16),
+            pltpu.VMEM((4, lists, TILE, cols), BF16),
+            pltpu.VMEM((4, rows, cols), BF16),
+            pltpu.VMEM((width, cols), BF16),
+            pltpu.VMEM((width, cols), BF16),
+            pltpu.VMEM((width, cols), BF16),
+            pltpu.VMEM((4, cols, cols), BF16),
+            pltpu.VMEM((rows, width), BF16),
+            pltpu.VMEM((rows, cols), BF16),
+            pltpu.VMEM((lists * TILE, cols), BF16),
+            pltpu.VMEM((lists * TILE, cols), BF16),
+            pltpu.VMEM((heads, rows, lists * TILE), F32),
+            dma((4,)),
+            dma((2,)), dma((2,)), dma((6,)), dma((6,)),
+            dma((4,)), dma((4,)),
+            dma((lists,)), dma((lists,)), dma((lists,)), dma((lists,)), dma((lists,)), dma((lists,)),
+            dma((heads,)), dma((heads,)), dma((heads,)), dma((heads,)), dma((heads,)), dma((heads,)),
+        ],
+        compiler_params=pltpu.CompilerParams(
+            collective_id=0, has_side_effects=True, vmem_limit_bytes=32 << 20
+        ),
+    )(
+        pattern, states, modulation, query_weight, key_weight, value_weight,
+        out_weight.reshape(4, cols, cols),
+    )
 
 
 def local(states, modulation, query_weight, key_weight, value_weight, out_weight, pattern):
@@ -70,6 +400,7 @@
 
 def solution(mesh):
     placed = (P("seq", "tp"), P(), P(None, "tp"), P(None, "tp"), P(None, "tp"), P(None, "tp"), P())
+    small = mesh.shape["seq"] == 8 and mesh.shape["tp"] == 4
     return jax.shard_map(
-        local, mesh=mesh, in_specs=placed, out_specs=P("seq", "tp"), check_vma=False
+        fused if small else local, mesh=mesh, in_specs=placed, out_specs=P("seq", "tp"), check_vma=False
     )

time: 109 us -> 52 us (0.48)
  waiting for transfers between devices: 59.2 us -> 0 us
  Pallas kernels: 0 us -> 43.2 us
  blocking collectives: 18.9 us -> 0 us
  between operations: 13.5 us -> 0.02 us
  matrix products: 4.7 us -> 0 us
  other arithmetic: 3.14 us -> 0 us
    all_gather x1 -> x0, waiting for transfers between devices: 59.2 us -> none  [local(): all_tiles = lax.all_gather(key_value, 'seq', axis=0, tiled=True)]
    pallas_call x0 -> x1, Pallas kernels: none -> 43.2 us  [fused(): pl.pallas_call(fused_kernel, out_shape=jax.ShapeDtypeStruct((rows, cols),...]
    all_gather x2 -> x0, blocking collectives: 18.9 us -> none  [the longest x1 10.3 us: local(): gathered = lax.all_gather(states, 'tp', axis=1, tiled=True)]
    gather x2 -> x0, local copies, waits for them, and re-layouts: 7.5 us -> none  [local(): jnp.take(tile_store, my_list, axis=0)]
    unnamed x13 -> x14, local copies, waits for them, and re-layouts: 0.73 us -> 8.19 us
    dot_general x6 -> x0, matrix products: 4.7 us -> none  [the longest x1 1.29 us: local(): jnp.dot(lax.all_gather(attended, 'tp', axis=1, tiled=True), out_weight, p...]
    reduce_sum x3 -> x0, other arithmetic: 1.18 us -> none  [the longest x1 0.65 us: attend(): weight_sum = jnp.sum(weights_full, axis=2)]
  transfers between devices with their start and end apart: 1 -> 0, of which waited for: 1 -> 0; matrix products, arithmetic and copies ran while one was open for 2% -> 0% of each run, Pallas kernels for 0% -> 0%
where the time goes in v1:
time: 52 us; the launch traced here: 51.4 us
  Pallas kernels  43.2 us (83%)
  local copies, waits for them, and re-layouts  8.19 us (16%)
    pallas_call x1, Pallas kernels, fused(): pl.pallas_call(fused_kernel, out_shape=jax.ShapeDtypeStruct((rows, cols),...  43.2 us
    unnamed x14, local copies, waits for them, and re-layouts  8.19 us

profile of v1, /device:TPU:0, one launch (start us, length us, event | category | flops | bytes accessed | tf_op | source)
XLA Modules:
  0.0 51.4 jit_solution(8132524140340825529)
XLA Ops:
  0.0 0.8 %copy.8.pat = s32[16,7]{1,0:T(8,128)S(1)} copy(s32[16,7]{0,1:T(8,128)} %param.13) | data formatting | bytes 896 | tf_op args[6]
  0.8 0.0 copy-start
  0.8 1.3 %copy-done = bf16[1536,384]{1,0:T(8,128)(2,1)S(1)} copy-done((bf16[1536,384]{1,0:T(8,128)(2,1)S(1)}, bf16[1536,384]{1,0:T(8,128)(2,1)}, u32[]{:S(2)}) %copy-start) | copy-done | bytes 1179672
  2.0 0.0 copy-start.1
  2.0 1.3 %copy-done.1 = bf16[1536,384]{1,0:T(8,128)(2,1)S(1)} copy-done((bf16[1536,384]{1,0:T(8,128)(2,1)S(1)}, bf16[1536,384]{1,0:T(8,128)(2,1)}, u32[]{:S(2)}) %copy-start.1) | copy-done | bytes 1179672
  3.3 0.0 copy-start.2
  3.3 1.3 %copy-done.2 = bf16[1536,384]{1,0:T(8,128)(2,1)S(1)} copy-done((bf16[1536,384]{1,0:T(8,128)(2,1)S(1)}, bf16[1536,384]{1,0:T(8,128)(2,1)}, u32[]{:S(2)}) %copy-start.2) | copy-done | bytes 1179672
  4.6 0.0 copy-start.3
  4.6 1.3 %copy-done.3 = bf16[1536,384]{1,0:T(8,128)(2,1)S(1)} copy-done((bf16[1536,384]{1,0:T(8,128)(2,1)S(1)}, bf16[1536,384]{1,0:T(8,128)(2,1)}, u32[]{:S(2)}) %copy-start.3) | copy-done | bytes 1179672
  5.8 0.0 copy-start.4
  5.8 0.9 %copy-done.4 = bf16[256,384]{1,0:T(8,128)(2,1)S(1)} copy-done((bf16[256,384]{1,0:T(8,128)(2,1)S(1)}, bf16[256,384]{1,0:T(8,128)(2,1)}, u32[]{:S(2)}) %copy-start.4) | copy-done | bytes 196632
  6.8 0.0 copy-start.5
  6.8 0.7 %copy-done.5 = f32[3,1536]{1,0:T(4,128)S(1)} copy-done((f32[3,1536]{1,0:T(4,128)S(1)}, f32[3,1536]{1,0:T(4,128)}, u32[]{:S(2)}) %copy-start.5) | copy-done | bytes 18456
  7.5 43.2 %shard_map.73 = bf16[256,384]{1,0:T(8,128)(2,1)S(1)} custom-call(s32[16,7]{1,0:T(8,128)S(1)} %copy.8.pat, bf16[256,384]{1,0:T(8,128)(2,1)S(1)} %copy-done.4, f32[3,1536]{1,0:T(4,128)S(1)} %copy-done.5, bf16[1536,384]{1,0:T(8,128)(2,1)S(1)} %copy-done, bf16[1536,384]{1,0:T(8,128)(2,1)S(1)} %copy-done.1, bf16[1536,384]{1,0:T(8,128)(2,1)S(1)} %copy-done.2, ...), custom_call_target="tpu_custom_call" | custom-call | tf_op jit(solution)/shard_map/pallas_call | solution.py:307
  50.7 0.7 %copy.10 = bf16[256,384]{1,0:T(8,128)(2,1)} copy(bf16[256,384]{1,0:T(8,128)(2,1)S(1)} %shard_map.73) | data formatting | bytes 393216
Async XLA Ops:
  0.8 1.3 %copy-start = (bf16[1536,384]{1,0:T(8,128)(2,1)S(1)}, bf16[1536,384]{1,0:T(8,128)(2,1)}, u32[]{:S(2)}) copy-start(bf16[1536,384]{1,0:T(8,128)(2,1)} %wq_hbm.1) | copy-start | bytes 3538948
  2.0 1.3 %copy-start.1 = (bf16[1536,384]{1,0:T(8,128)(2,1)S(1)}, bf16[1536,384]{1,0:T(8,128)(2,1)}, u32[]{:S(2)}) copy-start(bf16[1536,384]{1,0:T(8,128)(2,1)} %wk_hbm.1) | copy-start | bytes 3538948
  3.3 1.3 %copy-start.2 = (bf16[1536,384]{1,0:T(8,128)(2,1)S(1)}, bf16[1536,384]{1,0:T(8,128)(2,1)}, u32[]{:S(2)}) copy-start(bf16[1536,384]{1,0:T(8,128)(2,1)} %wv_hbm.1) | copy-start | bytes 3538948
  4.6 1.3 %copy-start.3 = (bf16[1536,384]{1,0:T(8,128)(2,1)S(1)}, bf16[1536,384]{1,0:T(8,128)(2,1)}, u32[]{:S(2)}) copy-start(bf16[1536,384]{1,0:T(8,128)(2,1)} %param.12) | copy-start | bytes 3538948
  5.8 0.9 %copy-start.4 = (bf16[256,384]{1,0:T(8,128)(2,1)S(1)}, bf16[256,384]{1,0:T(8,128)(2,1)}, u32[]{:S(2)}) copy-start(bf16[256,384]{1,0:T(8,128)(2,1)} %x_ref.1) | copy-start | bytes 589828
  6.8 0.7 %copy-start.5 = (f32[3,1536]{1,0:T(4,128)S(1)}, f32[3,1536]{1,0:T(4,128)}, u32[]{:S(2)}) copy-start(f32[3,1536]{1,0:T(4,128)} %mod.1) | copy-start | bytes 55300

commit v2 on v1

--- a/solution.py
+++ b/solution.py
@@ -15,8 +15,8 @@
 
 
 def fused_kernel(
-    pat, x_ref, mod, wq_hbm, wk_hbm, wv_hbm, wo_hbm, o_ref,
-    zb, ys, yr, gat, att, wq, wk, wv, wo, nb, qb, kb, vb, sc,
+    pat_hbm, x_hbm, mod_hbm, wq_hbm, wk_hbm, wv_hbm, wo_hbm, o_ref,
+    zb, ys, yr, gat, att, wq, wk, wv, wo, nb, qb, kb, vb, sc, acc_ref, pat, x_ref, mod,
     wsem, zup, zdn, zfw, zrv, ysn, yrv, xsn, xrv, csn, crv, dsn, drv,
     axs, axr, acs, acr, ads, adr,
 ):
@@ -44,9 +44,9 @@
 
     loads = [
         pltpu.make_async_copy(a, b, wsem.at[i])
-        for i, (a, b) in enumerate(((wq_hbm, wq), (wk_hbm, wk), (wv_hbm, wv), (wo_hbm, wo)))
+        for i, (a, b) in enumerate(((wq_hbm, wq), (wk_hbm, wk), (wv_hbm, wv), (wo_hbm, wo), (pat_hbm, pat), (x_hbm, x_ref), (mod_hbm, mod)))
     ]
-    for cpy in loads:
+    for cpy in (loads[5], loads[4], loads[6], *loads[:4]):
         cpy.start()
 
     barrier = pltpu.get_barrier_semaphore()
@@ -57,6 +57,7 @@
     def _():
         pl.semaphore_signal(barrier, inc=1, device_id=down, device_id_type=MESH)
 
+    loads[5].wait()
     pl.semaphore_wait(barrier, 4 + zz)
 
     def own(t):
@@ -116,9 +117,10 @@
         at = (z, 1 - zz, 2, 3)[i]
         return at if i == 0 else at + half * (3 - 2 * at)
 
-    lists = pat.shape[1]
-    mine = [pat[2 * seq, n] for n in range(lists)]
-    theirs = [pat[2 * (z * 2 + 1 - y), n] for n in range(lists)]
+    loads[4].wait()
+    lists = pat.shape[0]
+    mine = [pat[n, 2 * seq] for n in range(lists)]
+    theirs = [pat[n, 2 * (z * 2 + 1 - y)] for n in range(lists)]
 
     def count(entries, value):
         return sum(jnp.where(e == value, 1, 0) for e in entries)
@@ -195,12 +197,28 @@
         normalize(k, 0)
         project(k, TILE)
 
+    def y_arrive(i):
+        y_copy(i).wait_recv()
+
+    outer = zz == 0
+
     y_stage(0)
     for t in range(2):
         z_arrive(0, t)
         gat[tp, t] = x_ref[t * TILE : (t + 1) * TILE]
         x_arrive(t)
+
+        @pl.when(inner)
+        def _():
+            z_arrive(1, t)
+
     y_stage(1)
+
+    @pl.when(inner)
+    def _():
+        y_stage(2)
+
+    loads[6].wait()
     for t in range(2):
         rest_arrive(t)
         normalize(t, t * TILE)
@@ -209,33 +227,59 @@
     qb[...] = jnp.dot(nb[...], wq[...], preferred_element_type=F32).astype(BF16)
     project(0, 2 * TILE)
 
-    def y_arrive(i):
-        y_copy(i).wait_recv()
+    @pl.when(inner)
+    def _():
+        z_arrive(2, 0)
+        z_arrive(2, 1)
+        y_stage(3)
+
+    @pl.when(outer)
+    def _():
+        z_arrive(1, 0)
+        z_arrive(1, 1)
+        y_stage(2)
 
     y_arrive(0)
     y_arrive(1)
     slot_stage(0)
-    z_arrive(1, 0)
-    z_arrive(1, 1)
-    y_stage(2)
     slot_stage(1)
+
+    @pl.when(outer)
+    def _():
+        z_arrive(2, 0)
+
     x_arrive(2)
-    z_arrive(2, 0)
-    x_arrive(3)
-    z_arrive(2, 1)
-    y_stage(3)
     y_arrive(2)
     slot_stage(2)
+
+    @pl.when(outer)
+    def _():
+        z_arrive(2, 1)
+        y_stage(3)
+
     slot_stage(3)
+    x_arrive(3)
     attend(2)
+    attend(3)
     y_arrive(3)
     slot_stage(4)
     x_arrive(4)
-    attend(3)
+    attend(4)
     x_arrive(5)
-    attend(4)
+    attend(5)
+
+    early = (lists - 1) * TILE
+    parts = []
+    for h in range(heads):
+        lanes = slice(h * HD, (h + 1) * HD)
+        scores = sc[h, :, 0:early]
+        top = jnp.max(scores, axis=1, keepdims=True)
+        full = jnp.exp(scores - top)
+        total = jnp.sum(full, axis=1, keepdims=True)
+        summed = jnp.dot(full.astype(BF16), vb[0:early, lanes], preferred_element_type=F32)
+        acc_ref[h] = summed
+        parts.append((top, total))
     x_arrive(6)
-    attend(5)
     attend(6)
 
     def att_part(t, h):
@@ -252,10 +296,15 @@
 
     for h in range(heads):
         lanes = slice(h * HD, (h + 1) * HD)
-        scores = sc[h]
-        full = jnp.exp(scores - jnp.max(scores, axis=1, keepdims=True))
-        total = jnp.sum(full, axis=1, keepdims=True)
-        summed = jnp.dot(full.astype(BF16), vb[:, lanes], preferred_element_type=F32)
+        scores = sc[h, :, early:]
+        top, total = parts[h]
+        row_max = jnp.maximum(top, jnp.max(scores, axis=1, keepdims=True))
+        scale = jnp.exp(top - row_max)
+        full = jnp.exp(scores - row_max)
+        total = total * scale + jnp.sum(full, axis=1, keepdims=True)
+        summed = acc_ref[h] * scale + jnp.dot(
+            full.astype(BF16), vb[early:, lanes], preferred_element_type=F32
+        )
         att[tp, :, lanes] = (summed / total).astype(BF16)
         ax_copy(h).start()
         ac_copy(h).start()
@@ -302,12 +351,12 @@
     lists = pattern.shape[1]
     heads = cols // HD
     vmem = pl.BlockSpec(memory_space=pltpu.VMEM)
-    hbm = pl.BlockSpec(memory_space=pl.ANY)
+    hbm = pl.BlockSpec(memory_space=pltpu.HBM)
     dma = pltpu.SemaphoreType.DMA
     return pl.pallas_call(
         fused_kernel,
         out_shape=jax.ShapeDtypeStruct((rows, cols), BF16),
-        in_specs=[pl.BlockSpec(memory_space=pltpu.SMEM), vmem, vmem, hbm, hbm, hbm, hbm],
+        in_specs=[hbm] * 7,
         out_specs=vmem,
         scratch_shapes=[
             pltpu.VMEM((3, 2, TILE, cols), BF16),
@@ -324,17 +373,21 @@
             pltpu.VMEM((lists * TILE, cols), BF16),
             pltpu.VMEM((lists * TILE, cols), BF16),
             pltpu.VMEM((heads, rows, lists * TILE), F32),
-            dma((4,)),
+            pltpu.VMEM((heads, rows, HD), F32),
+            pltpu.SMEM(pattern.shape[::-1], jnp.int32),
+            pltpu.VMEM((rows, cols), BF16),
+            pltpu.VMEM(modulation.shape, F32),
+            dma((7,)),
             dma((2,)), dma((2,)), dma((6,)), dma((6,)),
             dma((4,)), dma((4,)),
             dma((lists,)), dma((lists,)), dma((lists,)), dma((lists,)), dma((lists,)), dma((lists,)),
             dma((heads,)), dma((heads,)), dma((heads,)), dma((heads,)), dma((heads,)), dma((heads,)),
         ],
         compiler_params=pltpu.CompilerParams(
-            collective_id=0, has_side_effects=True, vmem_limit_bytes=32 << 20
+            collective_id=0, has_side_effects=True, vmem_limit_bytes=60 * 1024 * 1024
         ),
     )(
-        pattern, states, modulation, query_weight, key_weight, value_weight,
+        pattern.T, states, modulation, query_weight, key_weight, value_weight,
         out_weight.reshape(4, cols, cols),
     )
 

time: 52 us -> 40.4 us (0.78)
  local copies, waits for them, and re-layouts: 8.19 us -> 1.62 us
  Pallas kernels: 43.2 us -> 38.5 us
    unnamed x14 -> x1, local copies, waits for them, and re-layouts: 8.19 us -> 1.62 us
    pallas_call x1, Pallas kernels: 43.2 us -> 38.5 us  [fused(): pl.pallas_call(fused_kernel, out_shape=jax.ShapeDtypeStruct((rows, cols),...]
where the time goes in v2:
time: 40.4 us; the launch traced here: 40.1 us
  Pallas kernels  38.5 us (95%)
  local copies, waits for them, and re-layouts  1.62 us (4%)
    pallas_call x1, Pallas kernels, fused(): pl.pallas_call(fused_kernel, out_shape=jax.ShapeDtypeStruct((rows, cols),...  38.5 us
    unnamed x1, local copies, waits for them, and re-layouts  1.62 us

profile of v2, /device:TPU:0, one launch (start us, length us, event | category | flops | bytes accessed | tf_op | source)
XLA Modules:
  0.0 40.1 jit_solution(830934863816250457)
XLA Ops:
  0.0 38.5 %shard_map.73 = bf16[256,384]{1,0:T(8,128)(2,1)} custom-call(s32[7,16]{1,0:T(8,128)} %bitcast.3, bf16[256,384]{1,0:T(8,128)(2,1)} %x_hbm.1, f32[3,1536]{1,0:T(4,128)} %mod_hbm.1, bf16[1536,384]{1,0:T(8,128)(2,1)} %wq_hbm.1, bf16[1536,384]{1,0:T(8,128)(2,1)} %wk_hbm.1, bf16[1536,384]{1,0:T(8,128)(2,1)} %wv_hbm.1, bf16[4,384,384]{2,1,0:T(8,128)(2,1)} %bitcast.2), custom_call_target="tpu_custom_call" | custom-call | tf_op jit(solution)/shard_map/pallas_call | solution.py:356
  38.5 1.6 %copy.9 = bf16[256,384]{1,0:T(8,128)(2,1)} copy(bf16[256,384]{1,0:T(8,128)(2,1)} %shard_map.73) | data formatting | bytes 393216
